TPU v7x, 128 devices: a whole 4x4x4 slice. The times are simulated.
128 devices in a mesh: ctx: 16 (over y_hi, x, core), head: 8 (over y_lo, z).
Axes of the slice: x: 4, y: 4 (y_hi: 2, y_lo: 2; y = y_hi * 2 + y_lo), z: 4, core: 2. Of those that a mesh axis runs over, the one named last changes fastest.
Arguments:
- block_order: int32 [32], replicated, may hold values from 0 to 31, each once
- queries: bfloat16 [3584, 64, 576], P('ctx', 'head'), may hold values from -10 to 10
- keys: bfloat16 [3584, 576], P('ctx'), may hold values from -4 to 4
- dout: bfloat16 [3584, 64, 512], P('ctx', 'head'), may hold values from -6 to 6
Outputs:
- grad_queries: bfloat16 [3584, 64, 576], P('ctx', 'head')
- grad_keys: float32 [3584, 576], P('ctx')
Inputs may be any that keep to these rules, and one draw needn't show every extreme that they name: block_order holds each of 0 to 31 once.
All inputs are finite; a program needn't handle non-finite values.
Results may differ from a plain program's by a relative error of at most 0.0048.
Values may be sent and summed in bfloat16 or wider, within the bound.
A program may use at most 64 MiB of HBM per device.

v0:
```python
import jax
import jax.numpy as jnp
from jax import lax
from jax.sharding import PartitionSpec as P

softmax_scale = 0.1352
masked_value = -1e30


def per_device(block_order, queries, keys, dout):
    token_count, head_count, key_width = queries.shape
    latent_width = dout.shape[2]
    block_rows = token_count // 2
    ctx_index = lax.axis_index("ctx")
    offsets = jnp.arange(block_rows, dtype=jnp.int32)
    all_positions = (block_order[:, None] * block_rows + offsets[None, :]).reshape(-1)
    own_positions = lax.dynamic_slice_in_dim(all_positions, ctx_index * token_count, token_count)
    row_positions = jnp.repeat(own_positions, head_count)
    query_last = jnp.max(own_positions)
    query_rows = queries.reshape(token_count * head_count, key_width)
    grad_rows = dout.reshape(token_count * head_count, latent_width)
    row_count = query_rows.shape[0]
    seq_length = token_count * lax.axis_size("ctx")
    contract_rows = (((0,), (0,)), ((), ()))

    def block_scores(key_block, key_pos):
        scores = (
            jnp.dot(query_rows, key_block.T, preferred_element_type=jnp.float32) * softmax_scale
        )
        return jnp.where(key_pos[None, :] <= row_positions[:, None], scores, masked_value)

    def split_piece(piece):
        count = piece.shape[0] // token_count
        return (
            piece.reshape(count, token_count, key_width),
            all_positions.reshape(count, token_count),
        )

    def make_second(peak, total, delta):

        def second_fold(carry, piece, start):
            grad_query, grad_keys = carry
            blocks, positions = split_piece(piece)

            def second_visit(accum, items):
                key_block, key_pos = items

                def second_compute(accum):
                    scores = block_scores(key_block, key_pos)
                    probs = jnp.exp(scores - peak[:, None]) / total[:, None]
                    grad_probs = jnp.dot(
                        grad_rows, key_block[:, :latent_width].T, preferred_element_type=jnp.float32
                    )
                    grad_scores = (probs * (grad_probs - delta[:, None])).astype(jnp.bfloat16)
                    probs_half = probs.astype(jnp.bfloat16)
                    accum = (
                        accum
                        + jnp.dot(grad_scores, key_block, preferred_element_type=jnp.float32)
                        * softmax_scale
                    )
                    key_part = (
                        lax.dot_general(
                            grad_scores,
                            query_rows,
                            contract_rows,
                            preferred_element_type=jnp.float32,
                        )
                        * softmax_scale
                    )
                    value_part = lax.dot_general(
                        probs_half, grad_rows, contract_rows, preferred_element_type=jnp.float32
                    )
                    return (
                        accum,
                        key_part + jnp.pad(value_part, ((0, 0), (0, key_width - latent_width))),
                    )

                def skip(accum):
                    return (accum, jnp.zeros((token_count, key_width), jnp.float32))

                return lax.cond(jnp.min(key_pos) <= query_last, second_compute, skip, accum)

            grad_query, key_terms = lax.scan(second_visit, grad_query, (blocks, positions))
            length = piece.shape[0]
            grad_keys = key_terms.reshape(length, key_width)
            return (grad_query, grad_keys)

        return second_fold

    start_state = (
        jnp.full((row_count,), masked_value, jnp.float32),
        jnp.zeros((row_count,), jnp.float32),
        jnp.zeros((row_count,), jnp.float32),
    )
    second_start = (
        jnp.zeros((row_count, key_width), jnp.float32),
        jnp.zeros((seq_length, key_width), jnp.float32),
    )
    carry = start_state
    blocks, positions = split_piece(lax.all_gather(keys, "ctx", axis=0, tiled=True))

    def first_visit(state, items):
        key_block, key_pos = items

        def first_compute(state):
            peak, total, weighted = state
            scores = block_scores(key_block, key_pos)
            grad_probs = jnp.dot(
                grad_rows, key_block[:, :latent_width].T, preferred_element_type=jnp.float32
            )
            new_peak = jnp.maximum(peak, jnp.max(scores, axis=1))
            factor = jnp.exp(peak - new_peak)
            weights = jnp.exp(scores - new_peak[:, None])
            total = total * factor + jnp.sum(weights, axis=1)
            weighted = weighted * factor + jnp.sum(weights * grad_probs, axis=1)
            return (new_peak, total, weighted)

        def keep(state):
            return state

        return (lax.cond(jnp.min(key_pos) <= query_last, first_compute, keep, state), None)

    carry, unused = lax.scan(first_visit, carry, (blocks, positions))
    peak, total, weighted = carry
    second_fold = make_second(peak, total, weighted / total)
    grad_query, grad_keys = second_fold(
        second_start, lax.all_gather(keys, "ctx", axis=0, tiled=True), jnp.int32(0)
    )
    grad_queries = grad_query.reshape(token_count, head_count, key_width).astype(jnp.bfloat16)
    own_terms = lax.psum_scatter(grad_keys, "ctx", scatter_dimension=0, tiled=True)
    key_result = lax.psum(own_terms, "head")
    return (grad_queries, key_result)


def solution(mesh):
    placed = (P(), P("ctx", "head", None), P("ctx", None), P("ctx", "head", None))
    return jax.shard_map(
        per_device,
        mesh=mesh,
        in_specs=placed,
        out_specs=(P("ctx", "head", None), P("ctx", None)),
        check_vma=False,
    )
```

profile of v0, /device:TPU:0, one launch (start us, length us, event | category | flops | bytes accessed | tf_op | source)
XLA Modules:
  0.0 600.2 jit_solution(2105240949158212985)
XLA Ops:
  9.9 60.6 %all-gather.2.cloned.1.call-done = bf16[3584,576]{1,0:T(8,128)(2,1)} async-done(((bf16[224,576]{1,0:T(8,128)(2,1)}), bf16[3584,576]{1,0:T(8,128)(2,1)}) %all-gather.2.cloned.1.call-update) | async-done | bytes 4128784 | tf_op jit(solution)/shard_map/all_gather | solution.py:127
  70.5 69.5 %while.31 = (s32[]{:T(128)}, f32[1792]{0:T(1024)S(1)}, f32[1792]{0:T(1024)S(1)}, f32[1792]{0:T(1024)S(1)}, s32[16,224]{1,0:T(8,128)S(1)}, /*index=5*/s32[]{:T(12...) while((s32[]{:T(128)}, f32[1792]{0:T(1024)S(1)}, ...), condition=%wide.region_8.9_spmd.clone, body=%wide.region_1.8_spmd.clone.sunk | while | flops 877082112 | bytes 17222444 | solution.py:123
  72.4 5.0 conditional.6
  82.9 5.0 conditional.6
  91.6 5.0 conditional.6
  92.8 2.7 fusion.26
  98.4 5.0 conditional.6
  99.7 2.7 fusion.26
  110.9 5.0 conditional.6
  119.6 5.0 conditional.6
  126.4 5.0 conditional.6
  133.2 5.0 conditional.6
  134.4 2.7 fusion.26
  142.3 136.9 %while.32 = (s32[]{:T(128)}, f32[1792,576]{0,1:T(8,128)}, f32[16,224,576]{2,1,0:T(8,128)}, s32[16,224]{1,0:T(8,128)S(1)}, s32[]{:T(128)}, /*index=5*/bf16[16,224...) while((s32[]{:T(128)}, f32[1792,576]{0,1:T(8,128)}, ...), condition=%wide.region_13.14_spmd.clone, body=%wide.region_9.13_spmd.clone.sunk | while | flops 2215284992 | bytes 68409680 | solution.py:83
  144.2 11.5 %conditional.7 = (f32[1792,576]{0,1:T(8,128)}, f32[1,224,576]{2,1,0:T(8,128)S(1)}) conditional(s32[]{:T(128)} %convert_element_type.32, f32[1792,576]{0,1:T(8,128)} %get-tuple-element.560, (s32[1,224]{1,0:T(1,128)S(1)}, s32[224]{0:T(256)S(1)}, bf16[16,224,576]{2,1,0:T(8,128)(2,1)}, s32[]{:T(128)}, bf16[1792,576]{1,0:T(8,128)(2,1)}, ...), branch_computations={%region_11.11_spmd, %region_12.12_spmd} | conditional | flops 2215284736 | bytes 67317608 | solution.py:81
  164.2 11.5 %conditional.7 = (f32[1792,576]{0,1:T(8,128)}, f32[1,224,576]{2,1,0:T(8,128)S(1)}) conditional(s32[]{:T(128)} %convert_element_type.32, f32[1792,576]{0,1:T(8,128)} %get-tuple-element.560, (s32[1,224]{1,0:T(1,128)S(1)}, s32[224]{0:T(256)S(1)}, bf16[16,224,576]{2,1,0:T(8,128)(2,1)}, s32[]{:T(128)}, bf16[1792,576]{1,0:T(8,128)(2,1)}, ...), branch_computations={%region_11.11_spmd, %region_12.12_spmd} | conditional | flops 2215284736 | bytes 67317608 | solution.py:81
  181.3 11.5 %conditional.7 = (f32[1792,576]{0,1:T(8,128)}, f32[1,224,576]{2,1,0:T(8,128)S(1)}) conditional(s32[]{:T(128)} %convert_element_type.32, f32[1792,576]{0,1:T(8,128)} %get-tuple-element.560, (s32[1,224]{1,0:T(1,128)S(1)}, s32[224]{0:T(256)S(1)}, bf16[16,224,576]{2,1,0:T(8,128)(2,1)}, s32[]{:T(128)}, bf16[1792,576]{1,0:T(8,128)(2,1)}, ...), branch_computations={%region_11.11_spmd, %region_12.12_spmd} | conditional | flops 2215284736 | bytes 67317608 | solution.py:81
  195.5 11.5 %conditional.7 = (f32[1792,576]{0,1:T(8,128)}, f32[1,224,576]{2,1,0:T(8,128)S(1)}) conditional(s32[]{:T(128)} %convert_element_type.32, f32[1792,576]{0,1:T(8,128)} %get-tuple-element.560, (s32[1,224]{1,0:T(1,128)S(1)}, s32[224]{0:T(256)S(1)}, bf16[16,224,576]{2,1,0:T(8,128)(2,1)}, s32[]{:T(128)}, bf16[1792,576]{1,0:T(8,128)(2,1)}, ...), branch_computations={%region_11.11_spmd, %region_12.12_spmd} | conditional | flops 2215284736 | bytes 67317608 | solution.py:81
  218.3 11.5 %conditional.7 = (f32[1792,576]{0,1:T(8,128)}, f32[1,224,576]{2,1,0:T(8,128)S(1)}) conditional(s32[]{:T(128)} %convert_element_type.32, f32[1792,576]{0,1:T(8,128)} %get-tuple-element.560, (s32[1,224]{1,0:T(1,128)S(1)}, s32[224]{0:T(256)S(1)}, bf16[16,224,576]{2,1,0:T(8,128)(2,1)}, s32[]{:T(128)}, bf16[1792,576]{1,0:T(8,128)(2,1)}, ...), branch_computations={%region_11.11_spmd, %region_12.12_spmd} | conditional | flops 2215284736 | bytes 67317608 | solution.py:81
  235.4 11.5 %conditional.7 = (f32[1792,576]{0,1:T(8,128)}, f32[1,224,576]{2,1,0:T(8,128)S(1)}) conditional(s32[]{:T(128)} %convert_element_type.32, f32[1792,576]{0,1:T(8,128)} %get-tuple-element.560, (s32[1,224]{1,0:T(1,128)S(1)}, s32[224]{0:T(256)S(1)}, bf16[16,224,576]{2,1,0:T(8,128)(2,1)}, s32[]{:T(128)}, bf16[1792,576]{1,0:T(8,128)(2,1)}, ...), branch_computations={%region_11.11_spmd, %region_12.12_spmd} | conditional | flops 2215284736 | bytes 67317608 | solution.py:81
  249.7 11.5 %conditional.7 = (f32[1792,576]{0,1:T(8,128)}, f32[1,224,576]{2,1,0:T(8,128)S(1)}) conditional(s32[]{:T(128)} %convert_element_type.32, f32[1792,576]{0,1:T(8,128)} %get-tuple-element.560, (s32[1,224]{1,0:T(1,128)S(1)}, s32[224]{0:T(256)S(1)}, bf16[16,224,576]{2,1,0:T(8,128)(2,1)}, s32[]{:T(128)}, bf16[1792,576]{1,0:T(8,128)(2,1)}, ...), branch_computations={%region_11.11_spmd, %region_12.12_spmd} | conditional | flops 2215284736 | bytes 67317608 | solution.py:81
  263.9 11.5 %conditional.7 = (f32[1792,576]{0,1:T(8,128)}, f32[1,224,576]{2,1,0:T(8,128)S(1)}) conditional(s32[]{:T(128)} %convert_element_type.32, f32[1792,576]{0,1:T(8,128)} %get-tuple-element.560, (s32[1,224]{1,0:T(1,128)S(1)}, s32[224]{0:T(256)S(1)}, bf16[16,224,576]{2,1,0:T(8,128)(2,1)}, s32[]{:T(128)}, bf16[1792,576]{1,0:T(8,128)(2,1)}, ...), branch_computations={%region_11.11_spmd, %region_12.12_spmd} | conditional | flops 2215284736 | bytes 67317608 | solution.py:81
  279.3 235.7 %reduce-scatter.2.cloned.1.call-done = f32[224,576]{1,0:T(8,128)} async-done(((f32[3584,576]{1,0:T(8,128)}), f32[224,576]{1,0:T(8,128)}) %reduce-scatter.2.cloned.1.call-update) | async-done | bytes 516112 | tf_op jit(solution)/shard_map/reduce_scatter | solution.py:130
  520.0 71.8 %all-reduce.3.cloned.1.call-done = f32[224,576]{1,0:T(8,128)} async-done(((f32[224,576]{1,0:T(8,128)}), f32[224,576]{1,0:T(8,128)}) %all-reduce.3.cloned.1.call-update) | async-done | bytes 516112 | tf_op jit(solution)/shard_map/psum | solution.py:131
  (296 shorter events, 169.5 us)
Async XLA Ops:
  7.2 63.4 %all-gather.2.cloned.1.call-start = ((), (), s32[]{:S(2)}) async-start(), calls=%async_computation.1 | async-start | bytes 4874240 | tf_op jit(solution)/shard_map/all_gather | solution.py:127
  7.9 507.1 %reduce-scatter.2.cloned.1.call-start = ((), (), s32[]{:S(2)}) async-start(), calls=%async_computation.2 | async-start | bytes 9748480 | tf_op jit(solution)/shard_map/reduce_scatter | solution.py:130
  73.6 2.7 copy-start.2
  84.1 2.7 copy-start.2
  92.8 2.7 copy-start.2
  99.6 2.7 copy-start.2
  112.1 2.7 copy-start.2
  120.8 2.7 copy-start.2
  127.6 2.7 copy-start.2
  134.4 2.7 copy-start.2
  140.1 2.2 copy-start.3
  150.3 2.2 copy-start
  170.2 2.2 copy-start
  187.4 2.2 copy-start
  201.6 2.2 copy-start
  224.4 2.2 copy-start
  227.9 1.9 copy-start.1
  241.5 2.2 copy-start
  245.0 1.9 copy-start.1
  255.8 2.2 copy-start
  259.3 1.9 copy-start.1
  270.0 2.2 copy-start
  273.5 1.9 copy-start.1
  279.2 312.6 %all-reduce.3.cloned.1.call-start = ((), (), s32[]{:S(2)}) async-start(), calls=%async_computation.3 | async-start | bytes 1146880 | tf_op jit(solution)/shard_map/psum | solution.py:131
  (12 other events, 20.9 us)
Sparse Core Ops, SparseCore 0:
  10.4 60.0 all-gather.1
  279.4 235.6 reduce-scatter.1
  517.5 74.2 all-reduce.2
where the time goes:
time: 604 us; the launch traced here: 600 us
  waiting for transfers between devices  369 us (61%)
  matrix products  76.1 us (13%)
  local copies, waits for them, and re-layouts  73.3 us (12%)
  loops' own time  41.3 us (7%)
  other arithmetic  26.7 us (4%)
  between operations  13.8 us (2%)
    reduce_scatter x1, waiting for transfers between devices, per_device(): lax.psum_scatter(grad_keys, 'ctx', scatter_dimension=0, tiled=True)  236 us
    psum x1, waiting for transfers between devices, per_device(): key_result = lax.psum(own_terms, 'head')  71.8 us
    all_gather x1, waiting for transfers between devices, per_device(): lax.all_gather(keys, 'ctx', axis=0, tiled=True)  60.6 us
    dot_general x16, matrix products, block_scores(): jnp.dot(query_rows, key_block.T, preferred_element_type=jnp.float32)  42 us
    cond x72, local copies, waits for them, and re-layouts  33.3 us
    another operation x1, loops' own time, second_fold(): lax.scan(second_visit, grad_query, (blocks, positions))  20.3 us
    another operation x1, loops' own time, per_device(): carry, unused = lax.scan(first_visit, carry, (blocks, positions))  19.4 us
    squeeze x16, local copies, waits for them, and re-layouts, per_device(): carry, unused = lax.scan(first_visit, carry, (blocks, positions))  15.8 us
  transfers between devices with their start and end apart: 3, of which 3 were waited for; matrix products, arithmetic and copies ran while one was open for 1% of the time, Pallas kernels for 0%

commit v1 on v0

--- a/solution.py
+++ b/solution.py
@@ -5,6 +5,12 @@
 
 softmax_scale = 0.1352
 masked_value = -1e30
+
+
+def shape_boxes_up(message):
+    u1 = jnp.stack([message for _ in range(jax.lax.axis_size("ctx"))], axis=0)
+    extra = jax.lax.all_to_all(u1, "ctx", 0, 0)
+    return jnp.concatenate(extra, axis=0)
 
 
 def per_device(block_order, queries, keys, dout):
@@ -123,9 +129,7 @@
     carry, unused = lax.scan(first_visit, carry, (blocks, positions))
     peak, total, weighted = carry
     second_fold = make_second(peak, total, weighted / total)
-    grad_query, grad_keys = second_fold(
-        second_start, lax.all_gather(keys, "ctx", axis=0, tiled=True), jnp.int32(0)
-    )
+    grad_query, grad_keys = second_fold(second_start, shape_boxes_up(keys), jnp.int32(0))
     grad_queries = grad_query.reshape(token_count, head_count, key_width).astype(jnp.bfloat16)
     own_terms = lax.psum_scatter(grad_keys, "ctx", scatter_dimension=0, tiled=True)
     key_result = lax.psum(own_terms, "head")

time: 604 us -> 634 us (1.050)
  waiting for transfers between devices: 369 us -> 385 us
  starting transfers between devices: 0.12 us -> 7.42 us
    all_gather x1, waiting for transfers between devices: 60.6 us -> 81.6 us  [per_device(): lax.all_gather(keys, 'ctx', axis=0, tiled=True)]
    all_to_all x0 -> x1, starting transfers between devices: none -> 7.29 us  [shape_boxes_up(): extra = jax.lax.all_to_all(u1, 'ctx', 0, 0)]
    cond x72 -> x56, local copies, waits for them, and re-layouts: 33.3 us -> 33.4 us
  transfers between devices with their start and end apart: 3 -> 4, of which waited for: 3 -> 3; matrix products, arithmetic and copies ran while one was open for 1% -> 10% of each run, Pallas kernels for 0% -> 0%
where the time goes in v1:
time: 634 us; the launch traced here: 629 us
  waiting for transfers between devices  385 us (61%)
  local copies, waits for them, and re-layouts  78.5 us (12%)
  matrix products  74.5 us (12%)
  loops' own time  42.1 us (7%)
  other arithmetic  28.2 us (4%)
  between operations  13.8 us (2%)
  starting transfers between devices  7.42 us (1%)
    reduce_scatter x1, waiting for transfers between devices, per_device(): lax.psum_scatter(grad_keys, 'ctx', scatter_dimension=0, tiled=True)  234 us
    all_gather x1, waiting for transfers between devices, per_device(): lax.all_gather(keys, 'ctx', axis=0, tiled=True)  81.6 us
    psum x1, waiting for transfers between devices, per_device(): key_result = lax.psum(own_terms, 'head')  69 us
    dot_general x16, matrix products, block_scores(): jnp.dot(query_rows, key_block.T, preferred_element_type=jnp.float32)  41 us
    cond x56, local copies, waits for them, and re-layouts  33.4 us
    another operation x1, loops' own time, per_device(): carry, unused = lax.scan(first_visit, carry, (blocks, positions))  20.5 us
    another operation x1, loops' own time, second_fold(): lax.scan(second_visit, grad_query, (blocks, positions))  20 us
    squeeze x16, local copies, waits for them, and re-layouts, per_device(): carry, unused = lax.scan(first_visit, carry, (blocks, positions))  15.8 us
  transfers between devices with their start and end apart: 4, of which 3 were waited for; matrix products, arithmetic and copies ran while one was open for 10% of the time, Pallas kernels for 0%

profile of v1, /device:TPU:0, one launch (start us, length us, event | category | flops | bytes accessed | tf_op | source)
XLA Modules:
  0.0 629.5 jit_solution(16193269083397886617)
XLA Ops:
  11.4 7.3 %all-to-all-start = ((bf16[16,224,576]{2,1,0:T(8,128)(2,1)}), bf16[16,224,576]{2,1,0:T(8,128)(2,1)}, u32[]{:S(2)}, u32[]{:S(2)}) async-start(bf16[16,224,576]{2,1,0:T(8,128)(2,1)} %stack.2), calls=%async_computation | async-start | bytes 9175040 | tf_op jit(solution)/shard_map/all_to_all | solution.py:12
  20.0 81.6 %all-gather.2.cloned.1.call-done = bf16[3584,576]{1,0:T(8,128)(2,1)} async-done(((bf16[224,576]{1,0:T(8,128)(2,1)}), bf16[3584,576]{1,0:T(8,128)(2,1)}) %all-gather.2.cloned.1.call-update) | async-done | bytes 4128784 | tf_op jit(solution)/shard_map/all_gather | solution.py:106
  101.6 69.8 %while.31 = (s32[]{:T(128)}, f32[1792]{0:T(1024)S(1)}, f32[1792]{0:T(1024)S(1)}, f32[1792]{0:T(1024)S(1)}, s32[16,224]{1,0:T(8,128)S(1)}, /*index=5*/s32[]{:T(12...) while((s32[]{:T(128)}, f32[1792]{0:T(1024)S(1)}, ...), condition=%wide.region_8.9_spmd.clone, body=%wide.region_1.8_spmd.clone.sunk | while | flops 877082112 | bytes 9882383 | solution.py:129
  103.5 4.8 conditional.6
  114.2 4.8 conditional.6
  123.0 4.8 conditional.6
  129.7 4.8 conditional.6
  142.4 4.8 conditional.6
  151.1 4.8 conditional.6
  157.9 4.8 conditional.6
  164.6 4.8 conditional.6
  173.6 136.9 %while.32 = (s32[]{:T(128)}, f32[1792,576]{0,1:T(8,128)}, f32[16,224,576]{2,1,0:T(8,128)}, s32[16,224]{1,0:T(8,128)S(1)}, s32[]{:T(128)}, /*index=5*/bf16[16,224...) while((s32[]{:T(128)}, f32[1792,576]{0,1:T(8,128)}, ...), condition=%wide.region_13.14_spmd.clone, body=%wide.region_9.13_spmd.clone.sunk | while | flops 2215284992 | bytes 68409680 | solution.py:89
  175.6 11.4 %conditional.7 = (f32[1792,576]{0,1:T(8,128)}, f32[1,224,576]{2,1,0:T(8,128)S(1)}) conditional(s32[]{:T(128)} %convert_element_type.32, f32[1792,576]{0,1:T(8,128)} %get-tuple-element.560, (s32[1,224]{1,0:T(1,128)S(1)}, s32[224]{0:T(256)S(1)}, bf16[16,224,576]{2,1,0:T(8,128)(2,1)}, s32[]{:T(128)}, bf16[1792,576]{1,0:T(8,128)(2,1)}, ...), branch_computations={%region_11.11_spmd, %region_12.12_spmd} | conditional | flops 2215284736 | bytes 67317608 | solution.py:87
  195.5 11.4 %conditional.7 = (f32[1792,576]{0,1:T(8,128)}, f32[1,224,576]{2,1,0:T(8,128)S(1)}) conditional(s32[]{:T(128)} %convert_element_type.32, f32[1792,576]{0,1:T(8,128)} %get-tuple-element.560, (s32[1,224]{1,0:T(1,128)S(1)}, s32[224]{0:T(256)S(1)}, bf16[16,224,576]{2,1,0:T(8,128)(2,1)}, s32[]{:T(128)}, bf16[1792,576]{1,0:T(8,128)(2,1)}, ...), branch_computations={%region_11.11_spmd, %region_12.12_spmd} | conditional | flops 2215284736 | bytes 67317608 | solution.py:87
  212.7 11.4 %conditional.7 = (f32[1792,576]{0,1:T(8,128)}, f32[1,224,576]{2,1,0:T(8,128)S(1)}) conditional(s32[]{:T(128)} %convert_element_type.32, f32[1792,576]{0,1:T(8,128)} %get-tuple-element.560, (s32[1,224]{1,0:T(1,128)S(1)}, s32[224]{0:T(256)S(1)}, bf16[16,224,576]{2,1,0:T(8,128)(2,1)}, s32[]{:T(128)}, bf16[1792,576]{1,0:T(8,128)(2,1)}, ...), branch_computations={%region_11.11_spmd, %region_12.12_spmd} | conditional | flops 2215284736 | bytes 67317608 | solution.py:87
  226.9 11.4 %conditional.7 = (f32[1792,576]{0,1:T(8,128)}, f32[1,224,576]{2,1,0:T(8,128)S(1)}) conditional(s32[]{:T(128)} %convert_element_type.32, f32[1792,576]{0,1:T(8,128)} %get-tuple-element.560, (s32[1,224]{1,0:T(1,128)S(1)}, s32[224]{0:T(256)S(1)}, bf16[16,224,576]{2,1,0:T(8,128)(2,1)}, s32[]{:T(128)}, bf16[1792,576]{1,0:T(8,128)(2,1)}, ...), branch_computations={%region_11.11_spmd, %region_12.12_spmd} | conditional | flops 2215284736 | bytes 67317608 | solution.py:87
  249.7 11.4 %conditional.7 = (f32[1792,576]{0,1:T(8,128)}, f32[1,224,576]{2,1,0:T(8,128)S(1)}) conditional(s32[]{:T(128)} %convert_element_type.32, f32[1792,576]{0,1:T(8,128)} %get-tuple-element.560, (s32[1,224]{1,0:T(1,128)S(1)}, s32[224]{0:T(256)S(1)}, bf16[16,224,576]{2,1,0:T(8,128)(2,1)}, s32[]{:T(128)}, bf16[1792,576]{1,0:T(8,128)(2,1)}, ...), branch_computations={%region_11.11_spmd, %region_12.12_spmd} | conditional | flops 2215284736 | bytes 67317608 | solution.py:87
  266.8 11.4 %conditional.7 = (f32[1792,576]{0,1:T(8,128)}, f32[1,224,576]{2,1,0:T(8,128)S(1)}) conditional(s32[]{:T(128)} %convert_element_type.32, f32[1792,576]{0,1:T(8,128)} %get-tuple-element.560, (s32[1,224]{1,0:T(1,128)S(1)}, s32[224]{0:T(256)S(1)}, bf16[16,224,576]{2,1,0:T(8,128)(2,1)}, s32[]{:T(128)}, bf16[1792,576]{1,0:T(8,128)(2,1)}, ...), branch_computations={%region_11.11_spmd, %region_12.12_spmd} | conditional | flops 2215284736 | bytes 67317608 | solution.py:87
  281.0 11.4 %conditional.7 = (f32[1792,576]{0,1:T(8,128)}, f32[1,224,576]{2,1,0:T(8,128)S(1)}) conditional(s32[]{:T(128)} %convert_element_type.32, f32[1792,576]{0,1:T(8,128)} %get-tuple-element.560, (s32[1,224]{1,0:T(1,128)S(1)}, s32[224]{0:T(256)S(1)}, bf16[16,224,576]{2,1,0:T(8,128)(2,1)}, s32[]{:T(128)}, bf16[1792,576]{1,0:T(8,128)(2,1)}, ...), branch_computations={%region_11.11_spmd, %region_12.12_spmd} | conditional | flops 2215284736 | bytes 67317608 | solution.py:87
  295.3 11.4 %conditional.7 = (f32[1792,576]{0,1:T(8,128)}, f32[1,224,576]{2,1,0:T(8,128)S(1)}) conditional(s32[]{:T(128)} %convert_element_type.32, f32[1792,576]{0,1:T(8,128)} %get-tuple-element.560, (s32[1,224]{1,0:T(1,128)S(1)}, s32[224]{0:T(256)S(1)}, bf16[16,224,576]{2,1,0:T(8,128)(2,1)}, s32[]{:T(128)}, bf16[1792,576]{1,0:T(8,128)(2,1)}, ...), branch_computations={%region_11.11_spmd, %region_12.12_spmd} | conditional | flops 2215284736 | bytes 67317608 | solution.py:87
  310.6 233.6 %reduce-scatter.2.cloned.1.call-done = f32[224,576]{1,0:T(8,128)} async-done(((f32[3584,576]{1,0:T(8,128)}), f32[224,576]{1,0:T(8,128)}) %reduce-scatter.2.cloned.1.call-update) | async-done | bytes 516112 | tf_op jit(solution)/shard_map/reduce_scatter | solution.py:134
  544.2 3.7 convert_element_type.22
  547.9 4.1 copy.7
  552.0 69.0 %all-reduce.3.cloned.1.call-done = f32[224,576]{1,0:T(8,128)} async-done(((f32[224,576]{1,0:T(8,128)}), f32[224,576]{1,0:T(8,128)}) %all-reduce.3.cloned.1.call-update) | async-done | bytes 516112 | tf_op jit(solution)/shard_map/psum | solution.py:135
  (285 shorter events, 174.8 us)
Async XLA Ops:
  7.2 94.4 %all-gather.2.cloned.1.call-start = ((), (), s32[]{:S(2)}) async-start(), calls=%async_computation.2 | async-start | bytes 4874240 | tf_op jit(solution)/shard_map/all_gather | solution.py:106
  11.4 7.5 %copy-start.4 = (s32[32]{0:T(128)S(1)}, s32[32]{0:T(128)}, u32[]{:S(2)}) copy-start(s32[32]{0:T(128)} %param.12) | copy-start | bytes 388
  11.4 90.2 %copy-start.2 = (bf16[224,8,512]{2,1,0:T(8,128)(2,1)S(1)}, bf16[224,8,512]{2,1,0:T(8,128)(2,1)}, u32[]{:S(2)}) copy-start(bf16[224,8,512]{2,1,0:T(8,128)(2,1)} %param.15) | copy-start | bytes 5505028
  11.4 160.1 %all-to-all-start = ((bf16[16,224,576]{2,1,0:T(8,128)(2,1)}), bf16[16,224,576]{2,1,0:T(8,128)(2,1)}, u32[]{:S(2)}, u32[]{:S(2)}) async-start(bf16[16,224,576]{2,1,0:T(8,128)(2,1)} %stack.2), calls=%async_computation | async-start | bytes 9175040 | tf_op jit(solution)/shard_map/all_to_all | solution.py:12
  18.7 525.5 %reduce-scatter.2.cloned.1.call-start = ((), (), s32[]{:S(2)}) async-start(), calls=%async_computation.3 | async-start | bytes 9748480 | tf_op jit(solution)/shard_map/reduce_scatter | solution.py:134
  179.9 1.6 copy-start.3
  181.6 2.2 copy-start
  185.1 1.9 copy-start.1
  199.9 1.6 copy-start.3
  201.6 2.2 copy-start
  205.1 1.9 copy-start.1
  218.7 2.2 copy-start
  222.2 1.9 copy-start.1
  232.9 2.2 copy-start
  236.4 1.9 copy-start.1
  255.8 2.2 copy-start
  259.2 1.9 copy-start.1
  272.9 2.2 copy-start
  276.3 1.9 copy-start.1
  287.1 2.2 copy-start
  290.6 1.9 copy-start.1
  301.3 2.2 copy-start
  304.8 1.9 copy-start.1
  310.5 310.5 %all-reduce.3.cloned.1.call-start = ((), (), s32[]{:S(2)}) async-start(), calls=%async_computation.4 | async-start | bytes 1146880 | tf_op jit(solution)/shard_map/psum | solution.py:135
  (6 other events, 9.9 us)
Sparse Core Ops, SparseCore 0:
  10.4 91.1 all-gather.1
  310.7 233.4 reduce-scatter.1
  546.7 74.2 all-reduce.2
